TPU v7x, 32 devices: a whole 2x2x4 slice. The times are simulated.
32 devices in a mesh: row: 8 (over y, x, core), col: 4 (over z).
Axes of the slice: x: 2, y: 2, z: 4, core: 2. Of those that a mesh axis runs over, the one named last changes fastest.
Arguments:
- right_sides: float32 [64, 32768], P(None, ('row', 'col'))
- diag_tiles: float32 [32, 1024, 1024], P(('row', 'col')), as said below
- low_rank: float32 [32, 4, 8, 2, 12, 1024], P('row', 'col'), as said below
- tile_ranks: int32 [32, 4, 8], P('row', 'col'), may hold values from 1 to 12, as said below
- inv_factor: float32 [256, 8, 128, 128], P(('row', 'col')), as said below
- sub_sizes: int32 [64], replicated, may hold values from 1 to 8, 256 in all
Outputs:
- solution: float32 [64, 32768], P(None, ('row', 'col'))
- residual: float32 [64, 32768], P(None, ('row', 'col'))
Inputs may be any that keep to these rules, and one draw needn't show every extreme that they name: `low_rank`: tile (j, i) holds the two factors of tile (i, j) in swapped order, and a diagonal tile's two factors are equal, so S is symmetric. `tile_ranks`: the rank of tile (i, j) equals that of tile (j, i); diagonal tiles have rank 12. `diag_tiles`: each tile is symmetric positive definite. `inv_factor`: the block at distance 0 of every span is lower triangular with a positive diagonal. `sub_sizes`: the sizes sum to 256.
All inputs are finite; a program needn't handle non-finite values.
Results may differ from a plain program's by a relative error of at most 0.0003.
Values sent between devices are 32-bit elements; how exact they have to be, the bound alone decides.
A program may use at most 128 MiB of HBM per device.

v0:
```python
import jax
import jax.numpy as jnp
from jax import lax
from jax.sharding import PartitionSpec as P

RANK = 12
finest = lax.Precision.HIGHEST


def shifted(x, axis, by):
    size = lax.axis_size(axis)
    pairs = [(i, i + by) for i in range(size) if 0 <= i + by < size]
    return lax.ppermute(x, axis, pairs)


def span_weights(sub_sizes, per_device, reach_len):
    span_ids = lax.axis_index(("row", "col")) * per_device + lax.iota(jnp.int32, per_device)
    ending = jnp.cumsum(sub_sizes)
    opening = ending - sub_sizes
    inside = (span_ids[:, None] >= opening[None, :]) & (span_ids[:, None] < ending[None, :])
    position = span_ids - jnp.sum(jnp.where(inside, opening[None, :], 0), axis=1)
    return (lax.iota(jnp.int32, reach_len)[None, :] <= position[:, None]).astype(jnp.float32)


def precondition(vector, inv_factor, weights):
    rhs_count, tile_len = vector.shape
    per_device = inv_factor.shape[0]
    reach_len = inv_factor.shape[1]
    span_len = inv_factor.shape[2]
    before = shifted(vector, ("row", "col"), 1)
    joined = jnp.concatenate([before, vector], axis=1).reshape(rhs_count, 2 * per_device, span_len)
    windows = jnp.stack(
        [joined[:, per_device - behind : 2 * per_device - behind] for behind in range(reach_len)],
        axis=2,
    )
    windows = windows * weights[None, :, :, None]
    forward = jnp.einsum("ltji,klti->klj", inv_factor, windows, precision=finest)
    spread = (
        jnp.einsum("ltji,klj->klti", inv_factor, forward, precision=finest)
        * weights[None, :, :, None]
    )
    placed = jnp.zeros_like(joined)
    for behind in range(reach_len):
        placed = placed + jnp.pad(
            spread[:, :, behind], ((0, 0), (per_device - behind, behind), (0, 0))
        )
    returned = shifted(placed[:, :per_device].reshape(rhs_count, tile_len), ("row", "col"), -1)
    return placed[:, per_device:].reshape(rhs_count, tile_len) + returned


def operate(vector, diag_tiles, low_rank, tile_ranks):
    rhs_count, tile_len = vector.shape
    tile_rows = low_rank.shape[0]
    local_part = jnp.dot(vector, diag_tiles[0], precision=finest)
    left_factor = low_rank[:, 0, :, 0]
    right_factor = low_rank[:, 0, :, 1]
    weights = (lax.iota(jnp.int32, RANK)[None, None, :] < tile_ranks[:, 0, :, None]).astype(
        jnp.float32
    )
    initial = jnp.zeros((rhs_count, tile_rows * tile_len), jnp.float32)
    piece = lax.all_gather(vector, "row", axis=1, tiled=True)
    count_tiles = piece.shape[1] // tile_len
    pieces = piece.reshape(rhs_count, count_tiles, tile_len)
    coeffs = (
        jnp.einsum("bmqt,pmt->bmqp", right_factor, pieces, precision=finest)
        * weights[:, :, :, None]
    )
    added = jnp.einsum("bmqt,bmqp->pbt", left_factor, coeffs, precision=finest)
    partial_rows = initial + added.reshape(rhs_count, tile_rows * tile_len)
    summed = lax.psum_scatter(partial_rows, "col", scatter_dimension=1, tiled=True)
    return local_part + summed


def solve_spd(matrix, target):
    factor = jnp.linalg.cholesky(matrix)
    return jax.scipy.linalg.cho_solve((factor, True), target)


def gram_of(first_block, second_block):
    return jnp.dot(first_block, second_block.T, precision=finest)


def apply_coeffs(coeffs, block_rows):
    return jnp.dot(coeffs.T, block_rows, precision=finest)


def global_sum(terms):
    return lax.psum((terms[0], terms[1]), ("row", "col"))


def body(right_sides, diag_tiles, low_rank, tile_ranks, inv_factor, sub_sizes):
    weights = span_weights(sub_sizes, inv_factor.shape[0], inv_factor.shape[1])
    residual = right_sides
    search = precondition(residual, inv_factor, weights)
    images = operate(search, diag_tiles, low_rank, tile_ranks)
    rho_now, curvature = global_sum((gram_of(search, residual), gram_of(search, images)))
    step_size = solve_spd(curvature, rho_now)
    solution = apply_coeffs(step_size, search)
    residual = residual - apply_coeffs(step_size, images)
    precond = precondition(residual, inv_factor, weights)
    product = operate(precond, diag_tiles, low_rank, tile_ranks)
    rho_next, self_term, cross_term = lax.psum(
        (gram_of(precond, residual), gram_of(precond, product), gram_of(search, product)),
        ("row", "col"),
    )
    beta_mix = solve_spd(rho_now, rho_next)
    curvature = (
        self_term
        + jnp.dot(cross_term.T, beta_mix, precision=finest)
        + jnp.dot(beta_mix.T, cross_term, precision=finest)
        + jnp.dot(beta_mix.T, jnp.dot(curvature, beta_mix, precision=finest), precision=finest)
    )
    search = precond + apply_coeffs(beta_mix, search)
    images = product + apply_coeffs(beta_mix, images)
    step_size = solve_spd(curvature, rho_next)
    solution = solution + apply_coeffs(step_size, search)
    residual = residual - apply_coeffs(step_size, images)
    return (solution, residual)


def solution(mesh):
    placed = (
        P(None, ("row", "col")),
        P(("row", "col"), None, None),
        P("row", "col", None, None, None, None),
        P("row", "col", None),
        P(("row", "col"), None, None, None),
        P(),
    )
    return jax.shard_map(
        body,
        mesh=mesh,
        in_specs=placed,
        out_specs=(P(None, ("row", "col")), P(None, ("row", "col"))),
        check_vma=False,
    )
```

profile of v0, /device:TPU:0, one launch (start us, length us, event | category | flops | bytes accessed | tf_op | source)
XLA Modules:
  0.0 335.0 jit_solution(9789738542311892284)
XLA Ops:
  7.2 5.0 %collective-permute-start = (f32[64,1024]{1,0:T(8,128)}, f32[64,1024]{1,0:T(8,128)S(1)}, u32[]{:S(2)}, u32[]{:S(2)}) collective-permute-start(f32[64,1024]{1,0:T(8,128)} %param.9), channel_id=1, source_target_pairs={{0,1},{1,2},{2,3},{3,4},{4,5},{5,6},{6,7},{7,8},{8,9},{9,10},{10,1... | collective-permute-start | bytes 786440 | tf_op jit(solution)/shard_map/ppermute | solution.py:13
  14.1 3.9 %collective-permute-done = f32[64,1024]{1,0:T(8,128)S(1)} collective-permute-done((f32[64,1024]{1,0:T(8,128)}, f32[64,1024]{1,0:T(8,128)S(1)}, u32[]{:S(2)}, u32[]{:S(2)}) %collective-permute-start) | collective-permute-done | bytes 262176 | tf_op jit(solution)/shard_map/ppermute | solution.py:13
  21.5 4.6 %fusion.20 = f32[64,8,128,1]{2,0,3,1:T(8,128)S(1)} fusion(f32[8,8,128,128]{3,2,1,0:T(8,128)S(1)} %copy-done, f32[64,8,8,128]{3,0,2,1:T(8,128)S(1)} %fusion.62, f32[8,8]{1,0:T(8,128)S(1)} %fusion.89), kind=kOutput, calls=%fused_computation.23 | convolution fusion | flops 805830656 | bytes 6553856 | tf_op jit(solution)/shard_map/ltji,klti->klj/dot_general | solution.py:37
  30.3 8.7 %collective-permute-done.1 = f32[64,1024]{1,0:T(8,128)S(1)} collective-permute-done((f32[64,1024]{1,0:T(8,128)S(1)}, f32[64,1024]{1,0:T(8,128)S(1)}, u32[]{:S(2)}, u32[]{:S(2)}) %collective-permute-start.1) | collective-permute-done | bytes 262176 | tf_op jit(solution)/shard_map/ppermute | solution.py:13
  40.5 6.1 %fusion.91 = (f32[4,1,8,1,12,1024]{5,3,4,2,1,0:T(1,128)S(1)}, f32[4,1,8,1,12,1024]{5,3,4,2,1,0:T(1,128)S(1)}) fusion(f32[4,1,8,2,12,1024]{5,3,4,2,1,0:T(2,128)} %param.11), kind=kLoop, calls=%fused_computation.139 | loop fusion | bytes 6291456 | tf_op jit(solution)/shard_map/slice | solution.py:55
  46.6 25.1 %all-gather.3.cloned.1.call-done = f32[64,8192]{1,0:T(8,128)} async-done(((f32[64,1024]{1,0:T(8,128)}), f32[64,8192]{1,0:T(8,128)}) %all-gather.3.cloned.1.call-update) | async-done | bytes 2097168 | tf_op jit(solution)/shard_map/all_gather | solution.py:61
  82.3 25.9 %reduce-scatter.3.cloned.1.call-done = f32[64,1024]{1,0:T(8,128)} async-done(((f32[64,4096]{1,0:T(8,128)}), f32[64,1024]{1,0:T(8,128)}) %reduce-scatter.3.cloned.1.call-update) | async-done | bytes 262160 | tf_op jit(solution)/shard_map/reduce_scatter | solution.py:70
  108.2 4.9 %fusion.26 = f32[64,1024]{1,0:T(8,128)S(1)} fusion(f32[64,1024]{1,0:T(8,128)} %reduce-scatter.3.cloned.1.call-done, f32[64,1024]{1,0:T(8,128)S(1)} %copy-done.2, f32[1,1024,1024]{2,1,0:T(8,128)} %param.10), kind=kOutput, calls=%fused_computation.25 | convolution fusion | flops 805371904 | bytes 4980736 | tf_op jit(solution)/shard_map/dot_general | solution.py:54
  114.1 39.2 %all-reduce.17 = (f32[64,64]{0,1:T(8,128)S(1)}, f32[64,64]{0,1:T(8,128)S(1)}) all-reduce(f32[64,64]{0,1:T(8,128)S(1)} %fusion.95, f32[64,64]{0,1:T(8,128)S(1)} %fusion.94), channel_id=1, replica_groups=mesh['row'=8,'col'=4] {'row','col'}, use_global_device_ids=true, to_apply=%region_6.8 | all-reduce | flops 8192 | bytes 65536 | tf_op jit(solution)/shard_map/psum | solution.py:88
  153.4 5.8 %cholesky.59 = f32[64,64]{1,0:T(8,128)S(1)} custom-call(f32[64,64]{1,0:T(8,128)S(1)} %fusion.87), custom_call_target="Cholesky" | custom-call | tf_op jit(solution)/shard_map/jit(cholesky)/cholesky | solution.py:75
  161.4 5.7 %custom-call.9 = f32[1,64,64]{1,2,0:T(8,128)S(1)} custom-call(f32[1,64,64]{2,1,0:T(8,128)} %fusion.70), custom_call_target="InvertDiagBlocksLowerTriangular" | custom-call | tf_op jit(solution)/shard_map/jit(_cho_solve)/triangular_solve | solution.py:76
  168.9 3.8 %collective-permute-start.2 = (f32[64,1024]{1,0:T(8,128)S(1)}, f32[64,1024]{1,0:T(8,128)S(1)}, u32[]{:S(2)}, u32[]{:S(2)}) collective-permute-start(f32[64,1024]{1,0:T(8,128)S(1)} %convolution_subtract_fusion.1), channel_id=1, source_target_pairs={{0,1},{1,2},{2,3},{3,4},{4,5},{5,6},{6,7},{7,8},{8,9},{9,10},{10,1... | collective-permute-start | bytes 786440 | tf_op jit(solution)/shard_map/ppermute | solution.py:13
  172.7 4.7 %collective-permute-done.2 = f32[64,1024]{1,0:T(8,128)S(1)} collective-permute-done((f32[64,1024]{1,0:T(8,128)S(1)}, f32[64,1024]{1,0:T(8,128)S(1)}, u32[]{:S(2)}, u32[]{:S(2)}) %collective-permute-start.2) | collective-permute-done | bytes 262176 | tf_op jit(solution)/shard_map/ppermute | solution.py:13
  179.9 4.6 %fusion.23 = f32[64,8,128,1]{2,0,3,1:T(8,128)S(1)} fusion(f32[8,8,128,128]{3,2,1,0:T(8,128)S(1)} %copy-done.1, f32[64,8,8,128]{3,0,2,1:T(8,128)S(1)} %fusion.54, f32[8,8]{1,0:T(8,128)S(1)} %copy-done.9), kind=kOutput, calls=%fused_computation.24 | convolution fusion | flops 805830656 | bytes 6553856 | tf_op jit(solution)/shard_map/ltji,klti->klj/dot_general | solution.py:37
  188.7 9.1 %collective-permute-done.3 = f32[64,1024]{1,0:T(8,128)S(1)} collective-permute-done((f32[64,1024]{1,0:T(8,128)S(1)}, f32[64,1024]{1,0:T(8,128)S(1)}, u32[]{:S(2)}, u32[]{:S(2)}) %collective-permute-start.3) | collective-permute-done | bytes 262176 | tf_op jit(solution)/shard_map/ppermute | solution.py:13
  198.8 29.4 %all-gather.5.cloned.1.call-done = f32[64,8192]{1,0:T(8,128)} async-done(((f32[64,1024]{1,0:T(8,128)}), f32[64,8192]{1,0:T(8,128)}) %all-gather.5.cloned.1.call-update) | async-done | bytes 2097168 | tf_op jit(solution)/shard_map/all_gather | solution.py:61
  231.0 3.6 %fusion.47 = f32[4,8,12,64]{3,2,0,1:T(8,128)S(1)} fusion(f32[4,1,8,1,12,1024]{5,3,4,2,1,0:T(1,128)S(1)} %get-tuple-element.10, f32[64,8,1024,1]{2,1,0,3:T(8,128)S(1)} %bitcast.312, f32[4,8,12]{2,0,1:T(4,128)S(1)} %fusion.88), kind=kOutput, calls=%fused_computation.35 | convolution fusion | flops 302014464 | bytes 3769856 | tf_op jit(solution)/shard_map/bmqt,pmt->bmqp/dot_general | solution.py:65
  237.4 5.8 %cholesky.70 = f32[64,64]{1,0:T(8,128)S(1)} custom-call(f32[64,64]{1,0:T(8,128)S(1)} %fusion.82), custom_call_target="Cholesky" | custom-call | tf_op jit(solution)/shard_map/jit(cholesky)/cholesky | solution.py:75
  244.6 4.9 %custom-call.10 = f32[1,64,64]{1,2,0:T(8,128)S(1)} custom-call(f32[1,64,64]{2,1,0:T(8,128)S(1)} %fusion.71), custom_call_target="InvertDiagBlocksLowerTriangular" | custom-call | tf_op jit(solution)/shard_map/jit(_cho_solve)/triangular_solve | solution.py:76
  249.9 15.0 %reduce-scatter.5.cloned.1.call-done = f32[64,1024]{1,0:T(8,128)} async-done(((f32[64,4096]{1,0:T(8,128)}), f32[64,1024]{1,0:T(8,128)}) %reduce-scatter.5.cloned.1.call-update) | async-done | bytes 262160 | tf_op jit(solution)/shard_map/reduce_scatter | solution.py:70
  264.8 4.8 %fusion.29 = f32[64,1024]{1,0:T(8,128)S(1)} fusion(f32[64,1024]{1,0:T(8,128)} %reduce-scatter.5.cloned.1.call-done, f32[64,1024]{1,0:T(8,128)S(1)} %copy-done.3, f32[1,1024,1024]{2,1,0:T(8,128)} %param.10), kind=kOutput, calls=%fused_computation.26 | convolution fusion | flops 805371904 | bytes 4980736 | tf_op jit(solution)/shard_map/dot_general | solution.py:54
  270.4 40.1 %all-reduce.16 = (f32[64,64]{1,0:T(8,128)S(1)}, f32[64,64]{1,0:T(8,128)S(1)}, f32[64,64]{0,1:T(8,128)S(1)}) all-reduce(f32[64,64]{1,0:T(8,128)S(1)} %fusion.98, f32[64,64]{1,0:T(8,128)S(1)} %fusion.97, f32[64,64]{0,1:T(8,128)S(1)} %fusion.96), channel_id=1, replica_groups=mesh['row'=8,'col'=4] {'row','col'}, use_global_device_ids=true, to_apply=%region_10.13 | all-reduce | flops 12288 | bytes 98304 | tf_op jit(solution)/shard_map/psum | solution.py:102
  312.8 5.8 %cholesky.81 = f32[64,64]{1,0:T(8,128)S(1)} custom-call(f32[64,64]{1,0:T(8,128)S(1)} %fusion.77), custom_call_target="Cholesky" | custom-call | tf_op jit(solution)/shard_map/jit(cholesky)/cholesky | solution.py:75
  320.0 4.9 %custom-call.11 = f32[1,64,64]{1,2,0:T(8,128)S(1)} custom-call(f32[1,64,64]{2,1,0:T(8,128)S(1)} %fusion.72), custom_call_target="InvertDiagBlocksLowerTriangular" | custom-call | tf_op jit(solution)/shard_map/jit(_cho_solve)/triangular_solve | solution.py:76
  (119 shorter events, 48.6 us)
Async XLA Ops:
  7.2 64.6 %all-gather.3.cloned.1.call-start = ((), (), s32[]{:S(2)}) async-start(), calls=%async_computation.2 | async-start | bytes 2359296 | tf_op jit(solution)/shard_map/all_gather | solution.py:61
  7.2 10.8 %collective-permute-start = (f32[64,1024]{1,0:T(8,128)}, f32[64,1024]{1,0:T(8,128)S(1)}, u32[]{:S(2)}, u32[]{:S(2)}) collective-permute-start(f32[64,1024]{1,0:T(8,128)} %param.9), channel_id=1, source_target_pairs={{0,1},{1,2},{2,3},{3,4},{4,5},{5,6},{6,7},{7,8},{8,9},{9,10},{10,1... | collective-permute-start | bytes 786440 | tf_op jit(solution)/shard_map/ppermute | solution.py:13
  14.1 12.0 %copy-start.8 = (f32[8,8]{1,0:T(8,128)}, f32[8,8]{1,0:T(8,128)S(1)}, u32[]{:S(2)}) copy-start(f32[8,8]{1,0:T(8,128)S(1)} %fusion.89) | copy-start | bytes 772
  19.3 2.2 copy-start
  28.7 11.6 %copy-start.10 = (s32[4,1,8]{2,1,0:T(1,128)S(1)}, s32[4,1,8]{2,1,0:T(1,128)}, u32[]{:S(2)}) copy-start(s32[4,1,8]{2,1,0:T(1,128)} %param.12) | copy-start | bytes 388
  29.0 10.0 %collective-permute-start.1 = (f32[64,1024]{1,0:T(8,128)S(1)}, f32[64,1024]{1,0:T(8,128)S(1)}, u32[]{:S(2)}, u32[]{:S(2)}) collective-permute-start(f32[64,1024]{1,0:T(8,128)S(1)} %bitcast.318), channel_id=1, source_target_pairs={{1,0},{2,1},{3,2},{4,3},{5,4},{6,5},{7,6},{8,7},{9,8},{10,9},{11,1... | collective-permute-start | bytes 786440 | tf_op jit(solution)/shard_map/ppermute | solution.py:13
  39.8 68.4 %reduce-scatter.3.cloned.1.call-start = ((), (), s32[]{:S(2)}) async-start(), calls=%async_computation.3 | async-start | bytes 1310720 | tf_op jit(solution)/shard_map/reduce_scatter | solution.py:70
  79.7 1.3 copy-start.2
  80.8 147.5 %all-gather.5.cloned.1.call-start = ((), (), s32[]{:S(2)}) async-start(), calls=%async_computation.4 | async-start | bytes 2359296 | tf_op jit(solution)/shard_map/all_gather | solution.py:61
  113.1 0.7 copy-start.4
  168.9 8.6 %copy-start.6 = (f32[64,1024]{1,0:T(8,128)}, f32[64,1024]{1,0:T(8,128)S(1)}, u32[]{:S(2)}) copy-start(f32[64,1024]{1,0:T(8,128)S(1)} %convolution_subtract_fusion.1) | copy-start | bytes 786436
  168.9 8.6 %collective-permute-start.2 = (f32[64,1024]{1,0:T(8,128)S(1)}, f32[64,1024]{1,0:T(8,128)S(1)}, u32[]{:S(2)}, u32[]{:S(2)}) collective-permute-start(f32[64,1024]{1,0:T(8,128)S(1)} %convolution_subtract_fusion.1), channel_id=1, source_target_pairs={{0,1},{1,2},{2,3},{3,4},{4,5},{5,6},{6,7},{7,8},{8,9},{9,10},{10,1... | collective-permute-start | bytes 786440 | tf_op jit(solution)/shard_map/ppermute | solution.py:13
  177.7 2.2 copy-start.1
  177.8 2.2 copy-start.9
  187.4 10.4 %collective-permute-start.3 = (f32[64,1024]{1,0:T(8,128)S(1)}, f32[64,1024]{1,0:T(8,128)S(1)}, u32[]{:S(2)}, u32[]{:S(2)}) collective-permute-start(f32[64,1024]{1,0:T(8,128)S(1)} %bitcast.319), channel_id=1, source_target_pairs={{1,0},{2,1},{3,2},{4,3},{5,4},{6,5},{7,6},{8,7},{9,8},{10,9},{11,1... | collective-permute-start | bytes 786440 | tf_op jit(solution)/shard_map/ppermute | solution.py:13
  198.6 66.3 %reduce-scatter.5.cloned.1.call-start = ((), (), s32[]{:S(2)}) async-start(), calls=%async_computation.5 | async-start | bytes 1310720 | tf_op jit(solution)/shard_map/reduce_scatter | solution.py:70
  236.2 13.3 %copy-start.3 = (f32[64,1024]{1,0:T(8,128)S(1)}, f32[64,1024]{1,0:T(8,128)}, u32[]{:S(2)}) copy-start(f32[64,1024]{1,0:T(8,128)} %bitcast_add_fusion) | copy-start | bytes 786436
  236.2 13.3 %copy-start.7 = (f32[64,1024]{1,0:T(8,128)S(1)}, f32[64,1024]{1,0:T(8,128)}, u32[]{:S(2)}) copy-start(f32[64,1024]{1,0:T(8,128)} %copy-done.6) | copy-start | bytes 786436
  249.9 61.0 %copy-start.5 = (f32[64,1024]{1,0:T(8,128)S(1)}, f32[64,1024]{1,0:T(8,128)}, u32[]{:S(2)}) copy-start(f32[64,1024]{1,0:T(8,128)} %copy-done.4) | copy-start | bytes 786436
Sparse Core Ops, SparseCore 0:
  39.9 31.7 all-gather.2
  80.9 27.2 reduce-scatter.2
  198.7 29.5 all-gather.4
  237.4 27.3 reduce-scatter.4
where the time goes:
time: 341 us; the launch traced here: 335 us
  waiting for transfers between devices  122 us (36%)
  blocking collectives  79.3 us (23%)
  matrix products  43.8 us (13%)
  other arithmetic  41.8 us (12%)
  local copies, waits for them, and re-layouts  20.9 us (6%)
  between operations  14.9 us (4%)
  starting transfers between devices  12.5 us (4%)
    all_gather x2, waiting for transfers between devices, operate(): piece = lax.all_gather(vector, 'row', axis=1, tiled=True)  54.5 us
    reduce_scatter x2, waiting for transfers between devices, operate(): lax.psum_scatter(partial_rows, 'col', scatter_dimension=1, tiled=True)  40.8 us
    psum x1, blocking collectives, body(): lax.psum((gram_of(precond, residual), gram_of(precond, product), gram_of(...  40.1 us
    psum x1, blocking collectives, global_sum(): return lax.psum((terms[0], terms[1]), ('row', 'col'))  39.2 us
    ppermute x4, waiting for transfers between devices, shifted(): return lax.ppermute(x, axis, pairs)  26.4 us
    another operation x9, other arithmetic, solve_spd(): factor = jnp.linalg.cholesky(matrix)  19.7 us
    another operation x6, other arithmetic, solve_spd(): return jax.scipy.linalg.cho_solve((factor, True), target)  18 us
    ppermute x4, starting transfers between devices, shifted(): return lax.ppermute(x, axis, pairs)  11.4 us
  transfers between devices with their start and end apart: 8, of which 8 were waited for; matrix products, arithmetic and copies ran while one was open for 7% of the time, Pallas kernels for 0%

commit v1 on v0

--- a/solution.py
+++ b/solution.py
@@ -58,7 +58,8 @@
         jnp.float32
     )
     initial = jnp.zeros((rhs_count, tile_rows * tile_len), jnp.float32)
-    piece = lax.all_gather(vector, "row", axis=1, tiled=True)
+    parts = lax.all_gather(vector, "row", axis=0, tiled=False)
+    piece = jnp.concatenate(parts, axis=1)
     count_tiles = piece.shape[1] // tile_len
     pieces = piece.reshape(rhs_count, count_tiles, tile_len)
     coeffs = (

time: 341 us -> 336 us (0.985)
  local copies, waits for them, and re-layouts: 20.9 us -> 15.2 us
    unnamed x42 -> x40, local copies, waits for them, and re-layouts: 10.7 us -> 5.16 us
where the time goes in v1:
time: 336 us; the launch traced here: 330 us
  waiting for transfers between devices  122 us (36%)
  blocking collectives  79.4 us (24%)
  matrix products  44.5 us (13%)
  other arithmetic  41.8 us (12%)
  local copies, waits for them, and re-layouts  15.2 us (5%)
  between operations  14.7 us (4%)
  starting transfers between devices  12.3 us (4%)
    all_gather x2, waiting for transfers between devices, operate(): parts = lax.all_gather(vector, 'row', axis=0, tiled=False)  54.6 us
    reduce_scatter x2, waiting for transfers between devices, operate(): lax.psum_scatter(partial_rows, 'col', scatter_dimension=1, tiled=True)  41 us
    psum x1, blocking collectives, body(): lax.psum((gram_of(precond, residual), gram_of(precond, product), gram_of(...  40 us
    psum x1, blocking collectives, global_sum(): return lax.psum((terms[0], terms[1]), ('row', 'col'))  39.4 us
    ppermute x4, waiting for transfers between devices, shifted(): return lax.ppermute(x, axis, pairs)  26.4 us
    another operation x9, other arithmetic, solve_spd(): factor = jnp.linalg.cholesky(matrix)  19.7 us
    another operation x6, other arithmetic, solve_spd(): return jax.scipy.linalg.cho_solve((factor, True), target)  18 us
    ppermute x4, starting transfers between devices, shifted(): return lax.ppermute(x, axis, pairs)  11.4 us
  transfers between devices with their start and end apart: 8, of which 8 were waited for; matrix products, arithmetic and copies ran while one was open for 7% of the time, Pallas kernels for 0%

profile of v1, /device:TPU:0, one launch (start us, length us, event | category | flops | bytes accessed | tf_op | source)
XLA Modules:
  0.0 330.1 jit_solution(17575768923699603502)
XLA Ops:
  7.2 5.0 %collective-permute-start = (f32[64,1024]{1,0:T(8,128)}, f32[64,1024]{1,0:T(8,128)S(1)}, u32[]{:S(2)}, u32[]{:S(2)}) collective-permute-start(f32[64,1024]{1,0:T(8,128)} %param.9), channel_id=1, source_target_pairs={{0,1},{1,2},{2,3},{3,4},{4,5},{5,6},{6,7},{7,8},{8,9},{9,10},{10,1... | collective-permute-start | bytes 786440 | tf_op jit(solution)/shard_map/ppermute | solution.py:13
  14.1 3.9 %collective-permute-done = f32[64,1024]{1,0:T(8,128)S(1)} collective-permute-done((f32[64,1024]{1,0:T(8,128)}, f32[64,1024]{1,0:T(8,128)S(1)}, u32[]{:S(2)}, u32[]{:S(2)}) %collective-permute-start) | collective-permute-done | bytes 262176 | tf_op jit(solution)/shard_map/ppermute | solution.py:13
  21.5 4.6 %fusion.18 = f32[64,8,128,1]{2,0,3,1:T(8,128)S(1)} fusion(f32[8,8,128,128]{3,2,1,0:T(8,128)S(1)} %copy-done, f32[64,8,8,128]{3,0,2,1:T(8,128)S(1)} %fusion.52, f32[8,8]{1,0:T(8,128)S(1)} %fusion.79), kind=kOutput, calls=%fused_computation.21 | convolution fusion | flops 805830656 | bytes 6553856 | tf_op jit(solution)/shard_map/ltji,klti->klj/dot_general | solution.py:37
  30.3 8.7 %collective-permute-done.1 = f32[64,1024]{1,0:T(8,128)S(1)} collective-permute-done((f32[64,1024]{1,0:T(8,128)S(1)}, f32[64,1024]{1,0:T(8,128)S(1)}, u32[]{:S(2)}, u32[]{:S(2)}) %collective-permute-start.1) | collective-permute-done | bytes 262176 | tf_op jit(solution)/shard_map/ppermute | solution.py:13
  40.4 6.1 %fusion.81 = (f32[4,1,8,1,12,1024]{5,3,4,2,1,0:T(1,128)S(1)}, f32[4,1,8,1,12,1024]{5,3,4,2,1,0:T(1,128)S(1)}) fusion(f32[4,1,8,2,12,1024]{5,3,4,2,1,0:T(2,128)} %param.11), kind=kLoop, calls=%fused_computation.137 | loop fusion | bytes 6291456 | tf_op jit(solution)/shard_map/slice | solution.py:55
  46.6 25.2 %all-gather.5.cloned.1.call-done = f32[512,1024]{1,0:T(8,128)} async-done(((f32[64,1024]{1,0:T(8,128)}), f32[512,1024]{1,0:T(8,128)}) %all-gather.5.cloned.1.call-update) | async-done | bytes 2097168 | tf_op jit(solution)/shard_map/all_gather | solution.py:61
  71.7 3.9 %fusion.33 = f32[4,8,12,64]{3,2,1,0:T(8,128)S(1)} fusion(f32[64,8,1024,1]{2,0,1,3:T(8,128)} %bitcast.320, f32[4,1,8,1,12,1024]{5,3,4,2,1,0:T(1,128)S(1)} %get-tuple-element.10, f32[4,8,12]{2,1,0:T(8,128)S(1)} %fusion.78), kind=kOutput, calls=%fused_computation.31 | convolution fusion | flops 302014464 | bytes 3769856 | tf_op jit(solution)/shard_map/bmqt,pmt->bmqp/dot_general | solution.py:66
  79.7 26.1 %reduce-scatter.3.cloned.1.call-done = f32[64,1024]{1,0:T(8,128)} async-done(((f32[64,4096]{1,0:T(8,128)}), f32[64,1024]{1,0:T(8,128)}) %reduce-scatter.3.cloned.1.call-update) | async-done | bytes 262160 | tf_op jit(solution)/shard_map/reduce_scatter | solution.py:71
  105.7 4.9 %fusion.24 = f32[64,1024]{1,0:T(8,128)S(1)} fusion(f32[64,1024]{1,0:T(8,128)} %reduce-scatter.3.cloned.1.call-done, f32[64,1024]{1,0:T(8,128)S(1)} %copy-done.2, f32[1,1024,1024]{2,1,0:T(8,128)} %param.10), kind=kOutput, calls=%fused_computation.23 | convolution fusion | flops 805371904 | bytes 4980736 | tf_op jit(solution)/shard_map/dot_general | solution.py:54
  111.7 39.4 %all-reduce.17 = (f32[64,64]{0,1:T(8,128)S(1)}, f32[64,64]{0,1:T(8,128)S(1)}) all-reduce(f32[64,64]{0,1:T(8,128)S(1)} %fusion.85, f32[64,64]{0,1:T(8,128)S(1)} %fusion.84), channel_id=1, replica_groups=mesh['row'=8,'col'=4] {'row','col'}, use_global_device_ids=true, to_apply=%region_6.8 | all-reduce | flops 8192 | bytes 65536 | tf_op jit(solution)/shard_map/psum | solution.py:89
  151.2 5.8 %cholesky.59 = f32[64,64]{1,0:T(8,128)S(1)} custom-call(f32[64,64]{1,0:T(8,128)S(1)} %fusion.77), custom_call_target="Cholesky" | custom-call | tf_op jit(solution)/shard_map/jit(cholesky)/cholesky | solution.py:76
  159.1 5.7 %custom-call.9 = f32[1,64,64]{1,2,0:T(8,128)S(1)} custom-call(f32[1,64,64]{2,1,0:T(8,128)} %fusion.60), custom_call_target="InvertDiagBlocksLowerTriangular" | custom-call | tf_op jit(solution)/shard_map/jit(_cho_solve)/triangular_solve | solution.py:77
  170.4 4.7 %collective-permute-done.2 = f32[64,1024]{1,0:T(8,128)S(1)} collective-permute-done((f32[64,1024]{1,0:T(8,128)S(1)}, f32[64,1024]{1,0:T(8,128)S(1)}, u32[]{:S(2)}, u32[]{:S(2)}) %collective-permute-start.2) | collective-permute-done | bytes 262176 | tf_op jit(solution)/shard_map/ppermute | solution.py:13
  177.6 4.6 %fusion.21 = f32[64,8,128,1]{2,0,3,1:T(8,128)S(1)} fusion(f32[8,8,128,128]{3,2,1,0:T(8,128)S(1)} %copy-done.1, f32[64,8,8,128]{3,0,2,1:T(8,128)S(1)} %fusion.44, f32[8,8]{1,0:T(8,128)S(1)} %copy-done.9), kind=kOutput, calls=%fused_computation.22 | convolution fusion | flops 805830656 | bytes 6553856 | tf_op jit(solution)/shard_map/ltji,klti->klj/dot_general | solution.py:37
  186.5 9.1 %collective-permute-done.3 = f32[64,1024]{1,0:T(8,128)S(1)} collective-permute-done((f32[64,1024]{1,0:T(8,128)S(1)}, f32[64,1024]{1,0:T(8,128)S(1)}, u32[]{:S(2)}, u32[]{:S(2)}) %collective-permute-start.3) | collective-permute-done | bytes 262176 | tf_op jit(solution)/shard_map/ppermute | solution.py:13
  196.6 29.4 %all-gather.7.cloned.1.call-done = f32[512,1024]{1,0:T(8,128)} async-done(((f32[64,1024]{1,0:T(8,128)}), f32[512,1024]{1,0:T(8,128)}) %all-gather.7.cloned.1.call-update) | async-done | bytes 2097168 | tf_op jit(solution)/shard_map/all_gather | solution.py:61
  226.0 3.9 %fusion.39 = f32[4,8,12,64]{3,2,1,0:T(8,128)S(1)} fusion(f32[64,8,1024,1]{2,0,1,3:T(8,128)} %bitcast.321, f32[4,1,8,1,12,1024]{5,3,4,2,1,0:T(1,128)S(1)} %get-tuple-element.10, f32[4,8,12]{2,1,0:T(8,128)S(1)} %fusion.78), kind=kOutput, calls=%fused_computation.33 | convolution fusion | flops 302014464 | bytes 3769856 | tf_op jit(solution)/shard_map/bmqt,pmt->bmqp/dot_general | solution.py:66
  232.7 5.8 %cholesky.70 = f32[64,64]{1,0:T(8,128)S(1)} custom-call(f32[64,64]{1,0:T(8,128)S(1)} %fusion.72), custom_call_target="Cholesky" | custom-call | tf_op jit(solution)/shard_map/jit(cholesky)/cholesky | solution.py:76
  239.9 4.9 %custom-call.10 = f32[1,64,64]{1,2,0:T(8,128)S(1)} custom-call(f32[1,64,64]{2,1,0:T(8,128)S(1)} %fusion.61), custom_call_target="InvertDiagBlocksLowerTriangular" | custom-call | tf_op jit(solution)/shard_map/jit(_cho_solve)/triangular_solve | solution.py:77
  245.2 15.0 %reduce-scatter.5.cloned.1.call-done = f32[64,1024]{1,0:T(8,128)} async-done(((f32[64,4096]{1,0:T(8,128)}), f32[64,1024]{1,0:T(8,128)}) %reduce-scatter.5.cloned.1.call-update) | async-done | bytes 262160 | tf_op jit(solution)/shard_map/reduce_scatter | solution.py:71
  260.1 4.8 %fusion.27 = f32[64,1024]{1,0:T(8,128)S(1)} fusion(f32[64,1024]{1,0:T(8,128)} %reduce-scatter.5.cloned.1.call-done, f32[64,1024]{1,0:T(8,128)S(1)} %copy-done.3, f32[1,1024,1024]{2,1,0:T(8,128)} %param.10), kind=kOutput, calls=%fused_computation.24 | convolution fusion | flops 805371904 | bytes 4980736 | tf_op jit(solution)/shard_map/dot_general | solution.py:54
  265.7 40.0 %all-reduce.16 = (f32[64,64]{1,0:T(8,128)S(1)}, f32[64,64]{1,0:T(8,128)S(1)}, f32[64,64]{0,1:T(8,128)S(1)}) all-reduce(f32[64,64]{1,0:T(8,128)S(1)} %fusion.88, f32[64,64]{1,0:T(8,128)S(1)} %fusion.87, f32[64,64]{0,1:T(8,128)S(1)} %fusion.86), channel_id=1, replica_groups=mesh['row'=8,'col'=4] {'row','col'}, use_global_device_ids=true, to_apply=%region_10.13 | all-reduce | flops 12288 | bytes 98304 | tf_op jit(solution)/shard_map/psum | solution.py:103
  308.1 5.8 %cholesky.81 = f32[64,64]{1,0:T(8,128)S(1)} custom-call(f32[64,64]{1,0:T(8,128)S(1)} %fusion.67), custom_call_target="Cholesky" | custom-call | tf_op jit(solution)/shard_map/jit(cholesky)/cholesky | solution.py:76
  315.3 4.9 %custom-call.11 = f32[1,64,64]{1,2,0:T(8,128)S(1)} custom-call(f32[1,64,64]{2,1,0:T(8,128)S(1)} %fusion.62), custom_call_target="InvertDiagBlocksLowerTriangular" | custom-call | tf_op jit(solution)/shard_map/jit(_cho_solve)/triangular_solve | solution.py:77
  (116 shorter events, 43.0 us)
Async XLA Ops:
  7.2 64.6 %all-gather.5.cloned.1.call-start = ((), (), s32[]{:S(2)}) async-start(), calls=%async_computation.4 | async-start | bytes 2359296 | tf_op jit(solution)/shard_map/all_gather | solution.py:61
  7.2 10.8 %collective-permute-start = (f32[64,1024]{1,0:T(8,128)}, f32[64,1024]{1,0:T(8,128)S(1)}, u32[]{:S(2)}, u32[]{:S(2)}) collective-permute-start(f32[64,1024]{1,0:T(8,128)} %param.9), channel_id=1, source_target_pairs={{0,1},{1,2},{2,3},{3,4},{4,5},{5,6},{6,7},{7,8},{8,9},{9,10},{10,1... | collective-permute-start | bytes 786440 | tf_op jit(solution)/shard_map/ppermute | solution.py:13
  14.1 12.0 %copy-start.8 = (f32[8,8]{1,0:T(8,128)}, f32[8,8]{1,0:T(8,128)S(1)}, u32[]{:S(2)}) copy-start(f32[8,8]{1,0:T(8,128)S(1)} %fusion.79) | copy-start | bytes 772
  19.3 2.2 copy-start
  28.7 11.6 %copy-start.10 = (s32[4,1,8]{2,1,0:T(1,128)S(1)}, s32[4,1,8]{2,1,0:T(1,128)}, u32[]{:S(2)}) copy-start(s32[4,1,8]{2,1,0:T(1,128)} %param.12) | copy-start | bytes 388
  29.0 10.0 %collective-permute-start.1 = (f32[64,1024]{1,0:T(8,128)S(1)}, f32[64,1024]{1,0:T(8,128)S(1)}, u32[]{:S(2)}, u32[]{:S(2)}) collective-permute-start(f32[64,1024]{1,0:T(8,128)S(1)} %bitcast.322), channel_id=1, source_target_pairs={{1,0},{2,1},{3,2},{4,3},{5,4},{6,5},{7,6},{8,7},{9,8},{10,9},{11,1... | collective-permute-start | bytes 786440 | tf_op jit(solution)/shard_map/ppermute | solution.py:13
  39.8 66.0 %reduce-scatter.3.cloned.1.call-start = ((), (), s32[]{:S(2)}) async-start(), calls=%async_computation.2 | async-start | bytes 1310720 | tf_op jit(solution)/shard_map/reduce_scatter | solution.py:71
  77.2 1.2 copy-start.2
  78.3 147.7 %all-gather.7.cloned.1.call-start = ((), (), s32[]{:S(2)}) async-start(), calls=%async_computation.5 | async-start | bytes 2359296 | tf_op jit(solution)/shard_map/all_gather | solution.py:61
  110.6 0.7 copy-start.4
  166.6 8.6 %copy-start.6 = (f32[64,1024]{1,0:T(8,128)}, f32[64,1024]{1,0:T(8,128)S(1)}, u32[]{:S(2)}) copy-start(f32[64,1024]{1,0:T(8,128)S(1)} %convolution_subtract_fusion.1) | copy-start | bytes 786436
  166.6 8.5 %collective-permute-start.2 = (f32[64,1024]{1,0:T(8,128)S(1)}, f32[64,1024]{1,0:T(8,128)S(1)}, u32[]{:S(2)}, u32[]{:S(2)}) collective-permute-start(f32[64,1024]{1,0:T(8,128)S(1)} %convolution_subtract_fusion.1), channel_id=1, source_target_pairs={{0,1},{1,2},{2,3},{3,4},{4,5},{5,6},{6,7},{7,8},{8,9},{9,10},{10,1... | collective-permute-start | bytes 786440 | tf_op jit(solution)/shard_map/ppermute | solution.py:13
  175.4 2.2 copy-start.1
  175.5 2.2 copy-start.9
  185.2 10.4 %collective-permute-start.3 = (f32[64,1024]{1,0:T(8,128)S(1)}, f32[64,1024]{1,0:T(8,128)S(1)}, u32[]{:S(2)}, u32[]{:S(2)}) collective-permute-start(f32[64,1024]{1,0:T(8,128)S(1)} %bitcast.323), channel_id=1, source_target_pairs={{1,0},{2,1},{3,2},{4,3},{5,4},{6,5},{7,6},{8,7},{9,8},{10,9},{11,1... | collective-permute-start | bytes 786440 | tf_op jit(solution)/shard_map/ppermute | solution.py:13
  196.3 63.8 %reduce-scatter.5.cloned.1.call-start = ((), (), s32[]{:S(2)}) async-start(), calls=%async_computation.3 | async-start | bytes 1310720 | tf_op jit(solution)/shard_map/reduce_scatter | solution.py:71
  231.5 13.3 %copy-start.3 = (f32[64,1024]{1,0:T(8,128)S(1)}, f32[64,1024]{1,0:T(8,128)}, u32[]{:S(2)}) copy-start(f32[64,1024]{1,0:T(8,128)} %bitcast_add_fusion) | copy-start | bytes 786436
  231.5 13.3 %copy-start.7 = (f32[64,1024]{1,0:T(8,128)S(1)}, f32[64,1024]{1,0:T(8,128)}, u32[]{:S(2)}) copy-start(f32[64,1024]{1,0:T(8,128)} %copy-done.6) | copy-start | bytes 786436
  245.2 61.0 %copy-start.5 = (f32[64,1024]{1,0:T(8,128)S(1)}, f32[64,1024]{1,0:T(8,128)}, u32[]{:S(2)}) copy-start(f32[64,1024]{1,0:T(8,128)} %copy-done.4) | copy-start | bytes 786436
Sparse Core Ops, SparseCore 0:
  39.9 31.7 all-gather.4
  78.4 27.2 reduce-scatter.2
  196.4 29.5 all-gather.6
  232.7 27.3 reduce-scatter.4
